TPU v7x, 256 devices: a whole 4x4x8 slice. The times are simulated.
256 devices in a mesh: tile: 4 (over y), proj: 16 (over x, z_hi, core), cuts: 4 (over z_lo).
Axes of the slice: x: 4, y: 4, z: 8 (z_hi: 2, z_lo: 4; z = z_hi * 4 + z_lo), core: 2. Of those that a mesh axis runs over, the one named last changes fastest.
Arguments:
- object_field: float32 [64, 2, 384, 2048], P(('proj', 'cuts'), None, None, 'tile'), may hold values from -5 to 5
- probe_field: float32 [2, 256, 256], replicated, may hold values from -6 to 6
- amplitudes: bfloat16 [64, 4, 6, 256, 256], P(('proj', 'cuts'), 'tile'), may hold values from 0 to 16
- pos_rows: int32 [64, 4, 6], P(('proj', 'cuts'), 'tile'), may hold values from 0 to 128
- pos_cols: int32 [64, 4, 6], P(('proj', 'cuts'), 'tile'), may hold values from 0 to 512
- counts: int32 [64, 4], P(('proj', 'cuts'), 'tile'), may hold values from 1 to 6, as said below
- admm_dual: float32 [64, 32, 2048], P(('proj', 'cuts'), None, 'tile'), may hold values from -4 to 4
- volume: float32 [32, 2048, 2048], P('cuts', ('tile', 'proj')), may hold values from -6 to 6
- proj_weights: bfloat16 [16, 2048, 2048], P(None, ('tile', 'proj')), may hold values from -0.125 to 0.125
- ray_weights: float32 [16, 2048], replicated, may hold values from -0.125 to 0.125
- angle_ids: int32 [64], replicated, may hold values from 0 to 15
Outputs:
- new_object: float32 [64, 2, 384, 2048], P(('proj', 'cuts'), None, None, 'tile')
- new_probe: float32 [2, 256, 256], replicated
- new_volume: float32 [32, 2048, 2048], P('cuts', ('tile', 'proj'))
Inputs may be any that keep to these rules, and one draw needn't show every extreme that they name: `counts`: every tile holds at least one live position and at most 6; exactly one tile of one projection holds 6, every other holds at most 3.
All inputs are finite; a program needn't handle non-finite values.
Results may differ from a plain program's by a relative error of at most 0.00095.
The roundings to bfloat16 on the way count: a program that leaves them out, or rounds other values in their place, can miss the bound.
Values may be sent and summed in bfloat16 or wider, within the bound.
A program may use at most 64 MiB of HBM per device.

v0:
```python
import math
import jax
import jax.numpy as jnp
from jax import lax
from jax.sharding import PartitionSpec as P

PB = 256
tomo_step = 1.0


def shifted(value, axis, steps):
    count = lax.axis_size(axis)
    leading, last = (max(0, -steps), min(count, count - steps))
    return lax.ppermute(value, axis, [(source, source + steps) for source in range(leading, last)])


def dft_tables(side):
    indices = jnp.arange(side, dtype=jnp.int32)
    products = indices[:, None] * indices[None, :] % side
    phase_angle = products.astype(jnp.float32) * (2.0 * math.pi / side)
    norm_factor = 1.0 / math.sqrt(side)
    return (
        (jnp.cos(phase_angle) * norm_factor).astype(jnp.bfloat16),
        (-jnp.sin(phase_angle) * norm_factor).astype(jnp.bfloat16),
    )


def matmul(left, right):
    return jnp.dot(left, right, preferred_element_type=jnp.float32)


def complex_matmul(left_real, left_imag, right_real, right_imag):
    out_real = matmul(left_real, right_real) - matmul(left_imag, right_imag)
    out_imag = matmul(left_real, right_imag) + matmul(left_imag, right_real)
    return (out_real, out_imag)


def patch_terms(patch_real, patch_imag, probe_real, probe_imag, amplitude, dft_real, dft_imag):
    wave_real = (probe_real * patch_real - probe_imag * patch_imag).astype(jnp.bfloat16)
    wave_imag = (probe_real * patch_imag + probe_imag * patch_real).astype(jnp.bfloat16)
    half_real, half_imag = complex_matmul(dft_real, dft_imag, wave_real, wave_imag)
    half_real = half_real.astype(jnp.bfloat16)
    half_imag = half_imag.astype(jnp.bfloat16)
    far_real, far_imag = complex_matmul(half_real, half_imag, dft_real, dft_imag)
    modulus = jnp.sqrt(far_real * far_real + far_imag * far_imag + 0.25)
    factor = amplitude.astype(jnp.float32) / modulus - 1.0
    diff_real = (far_real * factor).astype(jnp.bfloat16)
    diff_imag = (far_imag * factor).astype(jnp.bfloat16)
    conj_imag = -dft_imag
    back_half_real, back_half_imag = complex_matmul(dft_real, conj_imag, diff_real, diff_imag)
    back_half_real = back_half_real.astype(jnp.bfloat16)
    back_half_imag = back_half_imag.astype(jnp.bfloat16)
    back_real, back_imag = complex_matmul(back_half_real, back_half_imag, dft_real, conj_imag)
    object_real = probe_real * back_real + probe_imag * back_imag
    object_imag = probe_real * back_imag - probe_imag * back_real
    probe_grad_real = patch_real * back_real + patch_imag * back_imag
    probe_grad_imag = patch_real * back_imag - patch_imag * back_real
    energy = jnp.mean(patch_real * patch_real + patch_imag * patch_imag)
    return (
        jnp.stack([object_real, object_imag]),
        jnp.stack([probe_grad_real, probe_grad_imag]),
        energy,
    )


def tile_edges(values, offset):
    return shifted(values, "tile", offset)


def on_device(
    object_field,
    probe_field,
    amplitudes,
    pos_rows,
    pos_cols,
    counts,
    admm_dual,
    volume,
    proj_weights,
    ray_weights,
    angle_ids,
):
    half_side = PB // 2
    own_object = object_field[0]
    tile_cols = own_object.shape[2]
    from_left = tile_edges(own_object[:, :, tile_cols - half_side :], 1)
    from_right = tile_edges(own_object[:, :, :half_side], -1)
    extended = jnp.concatenate([from_left, own_object, from_right], axis=2)
    dft_real, dft_imag = dft_tables(PB)
    probe_real = probe_field[0]
    probe_imag = probe_field[1]
    zero_index = jnp.zeros((), jnp.int32)
    live_count = counts[0, 0]
    slot_total = amplitudes.shape[2]

    def slot_step(slot_index, state_tuple, weight):
        grad_sum, probe_sum, energy_sum = state_tuple
        anchor = (zero_index, pos_rows[0, 0, slot_index], pos_cols[0, 0, slot_index])
        object_patch = lax.dynamic_slice(extended, anchor, (2, PB, PB))
        object_part, probe_part, energy = patch_terms(
            object_patch[0],
            object_patch[1],
            probe_real,
            probe_imag,
            amplitudes[0, 0, slot_index],
            dft_real,
            dft_imag,
        )
        current = lax.dynamic_slice(grad_sum, anchor, (2, PB, PB))
        grad_sum = lax.dynamic_update_slice(grad_sum, current + weight * object_part, anchor)
        return (grad_sum, probe_sum + weight * probe_part, energy_sum + weight * energy)

    running = (
        jnp.zeros(extended.shape, jnp.float32),
        jnp.zeros((2, PB, PB), jnp.float32),
        jnp.zeros((), jnp.float32),
    )
    running = lax.fori_loop(
        0,
        slot_total,
        lambda slot_index, state_tuple: slot_step(
            slot_index, state_tuple, (slot_index < live_count).astype(jnp.float32)
        ),
        running,
    )
    grad_sum, probe_sum, energy_sum = running
    to_right_edge = tile_edges(grad_sum[:, :, :half_side], -1)
    to_left_edge = tile_edges(grad_sum[:, :, tile_cols + half_side :], 1)
    own_cells = grad_sum[:, :, half_side : half_side + tile_cols]
    own_cells = own_cells.at[:, :, :half_side].add(to_left_edge)
    own_cells = own_cells.at[:, :, tile_cols - half_side :].add(to_right_edge)
    probe_flat = jnp.concatenate([probe_sum.reshape(-1), jnp.broadcast_to(energy_sum, (128,))])
    probe_flat = lax.psum(probe_flat, ("tile", "proj", "cuts"))
    probe_grad = probe_flat[: probe_sum.size].reshape(probe_sum.shape)
    energy = probe_flat[probe_sum.size]
    new_probe = probe_field + probe_grad / (energy + 1e-05)
    probe_peak = jnp.max(probe_real * probe_real + probe_imag * probe_imag)
    new_object = (own_object + own_cells / (probe_peak + 1e-05))[None]
    slab_total = admm_dual.shape[1]
    first_row = (own_object.shape[1] - slab_total) // 2
    slab_values = new_object[:, 1, first_row : first_row + slab_total, :] + admm_dual
    arrived = lax.all_to_all(
        lax.all_to_all(slab_values, "proj", split_axis=2, concat_axis=0, tiled=True),
        "cuts",
        split_axis=1,
        concat_axis=0,
        tiled=True,
    )
    proj_count = lax.axis_size("proj")
    cuts_count = lax.axis_size("cuts")
    slab_dev = arrived.shape[1]
    u_share = arrived.shape[2]
    projections = proj_count * cuts_count
    arrived = arrived.reshape(cuts_count, proj_count, slab_dev, u_share).transpose(1, 0, 2, 3)
    target = (
        arrived.reshape(projections, slab_dev, u_share)
        .transpose(2, 0, 1)
        .reshape(u_share, projections * slab_dev)
    )
    angle_count = ray_weights.shape[0]
    x_share = volume.shape[1]
    width = volume.shape[2]
    onehot = (angle_ids[:, None] == jnp.arange(angle_count, dtype=jnp.int32)[None, :]).astype(
        jnp.float32
    )
    ray_table = jnp.dot(
        onehot, ray_weights, precision=lax.Precision.HIGHEST, preferred_element_type=jnp.float32
    )
    ray_sums = jnp.einsum("zxy,ay->azx", volume, ray_table, precision=lax.Precision.HIGHEST).astype(
        jnp.bfloat16
    )
    spread = onehot.astype(jnp.bfloat16)[:, :, None, None] * ray_sums[:, None, :, :]
    spread = spread.transpose(1, 3, 0, 2).reshape(angle_count * x_share, projections * slab_dev)
    weight_flat = proj_weights.reshape(angle_count * x_share, width)
    partial_term = lax.dot_general(
        weight_flat, spread, (((0,), (0,)), ((), ())), preferred_element_type=jnp.float32
    )
    own_rows = lax.psum_scatter(partial_term, ("tile", "proj"), scatter_dimension=0, tiled=True)
    own_residue = (own_rows - target).astype(jnp.bfloat16)
    residue = lax.all_gather(own_residue, ("tile", "proj"), axis=0, tiled=True)
    backproj = matmul(weight_flat, residue)
    backproj = backproj.reshape(angle_count, x_share, projections, slab_dev)
    back_sums = jnp.einsum("gxaz,ag->azx", backproj, onehot, precision=lax.Precision.HIGHEST)
    gradient = jnp.einsum("azx,ay->zxy", back_sums, ray_table, precision=lax.Precision.HIGHEST)
    new_volume = volume - tomo_step * gradient
    return (new_object, new_probe, new_volume)


def solution(mesh):
    in_specs = (
        P(("proj", "cuts"), None, None, "tile"),
        P(),
        P(("proj", "cuts"), "tile", None, None, None),
        P(("proj", "cuts"), "tile", None),
        P(("proj", "cuts"), "tile", None),
        P(("proj", "cuts"), "tile"),
        P(("proj", "cuts"), None, "tile"),
        P("cuts", ("tile", "proj"), None),
        P(None, ("tile", "proj"), None),
        P(),
        P(),
    )
    out_specs = (P(("proj", "cuts"), None, None, "tile"), P(), P("cuts", ("tile", "proj"), None))
    return jax.shard_map(
        on_device, mesh=mesh, in_specs=in_specs, out_specs=out_specs, check_vma=False
    )
```

profile of v0, /device:TPU:1, one launch (start us, length us, event | category | flops | bytes accessed | tf_op | source)
XLA Modules:
  0.0 628.5 jit_solution(16933225154168796481)
XLA Ops:
  8.1 3.2 copy.17
  13.5 4.0 collective-permute-start
  23.7 3.4 mul.431
  27.1 3.3 convolution_bitcast_fusion
  30.4 5.3 copy.31
  37.5 3.2 pad_maximum_fusion
  42.3 245.5 %while.23 = (s32[]{:T(128)}, f32[2,384,768]{1,2,0:T(8,128)}, f32[2,256,256]{2,1,0:T(8,128)}, f32[]{:T(128)}, s32[1,1,6]{2,1,0:T(1,128)S(1)}, /*index=5*/s32[1,1,...) while((s32[]{:T(128)}, f32[2,384,768]{1,2,0:T(8,128)}, ...), condition=%wide.region_2.3_spmd.clone.clone, body=%wide.region_0.2_spmd.clone.clone.sunk | while | flops 558956544 | bytes 21102956 | solution.py:118
  68.0 3.0 fusion.228
  75.4 6.6 %dynamic_update_slice.13 = f32[2,384,768]{1,2,0:T(8,128)} dynamic-update-slice(f32[2,384,768]{1,2,0:T(8,128)} %get-tuple-element.644, f32[2,256,256]{1,2,0:T(8,128)S(1)} %copy.50, s32[]{:T(128)} %constant.167.clone.1..sunk, s32[]{:T(128)S(6)} %select_n.153, s32[]{:T(128)S(6)} %select_n.154) | dynamic-update-slice | bytes 1048580 | tf_op jit(solution)/shard_map/while/body/eval_jaxpr/dynamic_update_slice | solution.py:110
  108.2 3.0 fusion.228
  116.7 6.0 dynamic_update_slice.13
  148.9 3.0 fusion.228
  157.4 6.2 dynamic_update_slice.13
  189.9 3.0 fusion.228
  198.3 6.3 dynamic_update_slice.13
  230.9 3.0 fusion.228
  239.3 6.6 %dynamic_update_slice.13 = f32[2,384,768]{1,2,0:T(8,128)} dynamic-update-slice(f32[2,384,768]{1,2,0:T(8,128)} %get-tuple-element.644, f32[2,256,256]{1,2,0:T(8,128)S(1)} %copy.50, s32[]{:T(128)} %constant.167.clone.1..sunk, s32[]{:T(128)S(6)} %select_n.153, s32[]{:T(128)S(6)} %select_n.154) | dynamic-update-slice | bytes 1048580 | tf_op jit(solution)/shard_map/while/body/eval_jaxpr/dynamic_update_slice | solution.py:110
  272.2 3.0 fusion.228
  280.6 6.3 %dynamic_update_slice.13 = f32[2,384,768]{1,2,0:T(8,128)} dynamic-update-slice(f32[2,384,768]{1,2,0:T(8,128)} %get-tuple-element.644, f32[2,256,256]{1,2,0:T(8,128)S(1)} %copy.50, s32[]{:T(128)} %constant.167.clone.1..sunk, s32[]{:T(128)S(6)} %select_n.153, s32[]{:T(128)S(6)} %select_n.154) | dynamic-update-slice | bytes 1048580 | tf_op jit(solution)/shard_map/while/body/eval_jaxpr/dynamic_update_slice | solution.py:110
  289.7 5.9 collective-permute-start.2
  300.1 2.7 collective-permute-done.2
  303.9 3.2 collective-permute-done.3
  313.5 22.6 %all_to_all.27 = f32[16,1,1024]{2,1,0:T(1,128)S(1)} all-to-all(f32[16,1,1024]{2,1,0:T(1,128)S(1)} %reshape.139), channel_id=1, replica_groups=mesh['tile'=4,'proj'=16,'cuts'=4] {'proj'}, dimensions={0} | all-to-all | bytes 131072 | tf_op jit(solution)/shard_map/all_to_all | solution.py:143
  340.0 3.3 all-to-all-start.1
  344.5 3.3 all-to-all-done.1
  348.8 102.0 %reduce-scatter.4.cloned.1.call-done = f32[32,512]{1,0:T(8,128)} async-done(((f32[2048,512]{1,0:T(8,128)}), f32[32,512]{1,0:T(8,128)}) %reduce-scatter.4.cloned.1.call-update) | async-done | bytes 65552
  452.6 145.6 %all-reduce.3.cloned.1.call-done = f32[131200]{0:T(1024)} async-done(((f32[131200]{0:T(1024)}), f32[131200]{0:T(1024)}) %all-reduce.3.cloned.1.call-update) | async-done | bytes 524816 | tf_op jit(solution)/shard_map/psum | solution.py:133
  604.0 3.0 copy.28
  607.0 2.9 convolution_bitcast_fusion.2
  609.9 2.5 reshape.131
  612.4 3.8 fusion.126
  616.4 4.7 convolution_subtract_fusion.4
  (229 shorter events, 197.1 us)
Async XLA Ops:
  8.0 19.1 %copy-start = (bf16[16,32,2048]{2,1,0:T(8,128)(2,1)S(1)}, bf16[16,32,2048]{2,1,0:T(8,128)(2,1)}, u32[]{:S(2)}) copy-start(bf16[16,32,2048]{2,1,0:T(8,128)(2,1)} %param.25) | copy-start | bytes 6291460
  8.0 10.8 %copy-start.13 = (s32[64]{0:T(128)S(1)}, s32[64]{0:T(128)}, u32[]{:S(2)}) copy-start(s32[64]{0:T(128)} %param.27) | copy-start | bytes 772
  8.0 10.9 %copy-start.9 = (f32[16,2048]{1,0:T(8,128)S(1)}, f32[16,2048]{1,0:T(8,128)}, u32[]{:S(2)}) copy-start(f32[16,2048]{1,0:T(8,128)} %param.26) | copy-start | bytes 393220
  8.0 442.8 %reduce-scatter.4.cloned.1.call-start = ((), (), s32[]{:S(2)}) async-start(), calls=%async_computation.5 | async-start | bytes 4259840
  11.2 8.9 %copy-start.3 = (f32[8,32,2048]{2,1,0:T(8,128)S(1)}, f32[8,32,2048]{2,1,0:T(8,128)}, u32[]{:S(2)}) copy-start(f32[8,32,2048]{2,1,0:T(8,128)} %param.24) | copy-start | bytes 6291460
  13.5 24.0 %collective-permute-start = (f32[2,384,128]{1,2,0:T(8,128)}, f32[2,384,128]{1,2,0:T(8,128)S(1)}, u32[]{:S(2)}, u32[]{:S(2)}) collective-permute-start(f32[2,384,128]{1,2,0:T(8,128)} %get-tuple-element.528), channel_id=1, source_target_pairs={{0,64},{64,128},{128,192},{1,65},{65,129},{129,193},{2,66},{66,130... | collective-permute-start | bytes 1179656 | tf_op jit(solution)/shard_map/ppermute | solution.py:14
  17.6 19.9 %collective-permute-start.1 = (f32[2,384,128]{1,2,0:T(8,128)}, f32[2,384,128]{1,2,0:T(8,128)}, u32[]{:S(2)}, u32[]{:S(2)}) collective-permute-start(f32[2,384,128]{1,2,0:T(8,128)} %get-tuple-element.529), channel_id=1, source_target_pairs={{64,0},{128,64},{192,128},{65,1},{129,65},{193,129},{66,2},{130,66... | collective-permute-start | bytes 1179656 | tf_op jit(solution)/shard_map/ppermute | solution.py:14
  19.4 0.8 copy-start.7
  35.7 1.0 copy-start.5
  40.7 1.6 copy-start.11
  40.7 1.6 copy-start.12
  42.2 254.7 %copy-start.10 = (f32[1,32,512]{2,1,0:T(8,128)S(1)}, f32[1,32,512]{2,1,0:T(8,128)}, u32[]{:S(2)}) copy-start(f32[1,32,512]{2,1,0:T(8,128)} %param.23) | copy-start | bytes 196612
  287.7 9.4 %copy-start.6 = (f32[2,256,256]{2,1,0:T(8,128)S(1)}, f32[2,256,256]{2,1,0:T(8,128)}, u32[]{:S(2)}) copy-start(f32[2,256,256]{2,1,0:T(8,128)} %param.18) | copy-start | bytes 1572868
  289.7 13.1 %collective-permute-start.2 = (f32[2,384,128]{1,2,0:T(8,128)}, f32[2,384,128]{1,2,0:T(8,128)}, u32[]{:S(2)}, u32[]{:S(2)}) collective-permute-start(f32[2,384,128]{1,2,0:T(8,128)} %get-tuple-element.527), channel_id=1, source_target_pairs={{0,64},{64,128},{128,192},{1,65},{65,129},{129,193},{2,66},{66,130... | collective-permute-start | bytes 1179656 | tf_op jit(solution)/shard_map/ppermute | solution.py:14
  295.7 11.4 %collective-permute-start.3 = (f32[2,384,128]{1,2,0:T(8,128)S(1)}, f32[2,384,128]{1,2,0:T(8,128)}, u32[]{:S(2)}, u32[]{:S(2)}) collective-permute-start(f32[2,384,128]{1,2,0:T(8,128)S(1)} %get-tuple-element.526), channel_id=1, source_target_pairs={{64,0},{128,64},{192,128},{65,1},{129,65},{193,129},{66,2},{130,66... | collective-permute-start | bytes 1179656 | tf_op jit(solution)/shard_map/ppermute | solution.py:14
  298.4 9.8 %copy-start.1 = (f32[1,2,384,512]{2,3,1,0:T(8,128)S(1)}, f32[1,2,384,512]{2,3,1,0:T(8,128)}, u32[]{:S(2)}) copy-start(f32[1,2,384,512]{2,3,1,0:T(8,128)} %copy.17) | copy-start | bytes 4718596
  308.4 1.1 copy-start.4
  309.5 33.8 %copy-start.2 = (f32[2,256,256]{2,1,0:T(8,128)S(1)}, f32[2,256,256]{2,1,0:T(8,128)}, u32[]{:S(2)}) copy-start(f32[2,256,256]{2,1,0:T(8,128)} %get-tuple-element.383) | copy-start | bytes 1572868
  340.0 7.9 %all-to-all-start.1 = ((f32[4,1,4096]{2,1,0:T(1,128)}), f32[4,1,4096]{2,1,0:T(1,128)S(1)}, u32[]{:S(2)}, u32[]{:S(2)}) async-start(f32[4,1,4096]{2,1,0:T(1,128)} %reshape.141), calls=%async_computation.1 | async-start | bytes 131072 | tf_op jit(solution)/shard_map/all_to_all | solution.py:142
  343.3 254.9 %all-reduce.3.cloned.1.call-start = ((), (), s32[]{:S(2)}) async-start(), calls=%async_computation.3 | async-start | bytes 1056768 | tf_op jit(solution)/shard_map/psum | solution.py:133
  344.5 262.5 %all-gather.2.cloned.1.call-start = ((), (), s32[]{:S(2)}) async-start(), calls=%async_computation.4 | async-start | bytes 2129920 | tf_op jit(solution)/shard_map/all_gather | solution.py:180
  612.4 4.0 copy-start.8
Sparse Core Ops, SparseCore 0:
  35.8 414.9 reduce-scatter.3
  454.3 86.0 all-gather.1
Sparse Core Ops, SparseCore 1:
  349.8 248.3 all-reduce.2
where the time goes:
time: 632 us; the launch traced here: 629 us
  waiting for transfers between devices  257 us (41%)
  matrix products  143 us (23%)
  local copies, waits for them, and re-layouts  99.8 us (16%)
  other arithmetic  42.6 us (7%)
  loops' own time  30.5 us (5%)
  blocking collectives  22.6 us (4%)
  between operations  17.1 us (3%)
  starting transfers between devices  16 us (3%)
    psum x1, waiting for transfers between devices, on_device(): probe_flat = lax.psum(probe_flat, ('tile', 'proj', 'cuts'))  146 us
    dot_general x97, matrix products, matmul(): return jnp.dot(left, right, preferred_element_type=jnp.float32)  129 us
    unnamed x4, waiting for transfers between devices  102 us
    dynamic_update_slice x12, local copies, waits for them, and re-layouts, slot_step(): lax.dynamic_update_slice(grad_sum, current + weight * object_part, anchor)  39.1 us
    another operation x1, loops' own time, on_device(): lax.fori_loop(0, slot_total, lambda slot_index, state_tuple: slot_step(sl...  30.5 us
    all_to_all x1, blocking collectives, on_device(): lax.all_to_all(slab_values, 'proj', split_axis=2, concat_axis=0, tiled=True)  22.6 us
    unnamed x40, local copies, waits for them, and re-layouts  18.8 us
  transfers between devices with their start and end apart: 8, of which 5 were waited for; matrix products, arithmetic and copies ran while one was open for 42% of the time, Pallas kernels for 0%

commit v1 on v0

--- a/solution.py
+++ b/solution.py
@@ -140,7 +140,12 @@
     first_row = (own_object.shape[1] - slab_total) // 2
     slab_values = new_object[:, 1, first_row : first_row + slab_total, :] + admm_dual
     arrived = lax.all_to_all(
-        lax.all_to_all(slab_values, "proj", split_axis=2, concat_axis=0, tiled=True),
+        jnp.concatenate(
+            lax.all_to_all(
+                jnp.stack(jnp.split(slab_values, lax.axis_size("proj"), axis=2)), "proj", 0, 0
+            ),
+            axis=0,
+        ),
         "cuts",
         split_axis=1,
         concat_axis=0,

time: 632 us -> 610 us (0.965)
  local copies, waits for them, and re-layouts: 99.8 us -> 74.5 us
  matrix products: 143 us -> 150 us
    unnamed x4, waiting for transfers between devices: 102 us -> 122 us
    psum x1, waiting for transfers between devices: 146 us -> 128 us  [on_device(): probe_flat = lax.psum(probe_flat, ('tile', 'proj', 'cuts'))]
    add x6 -> x1, other arithmetic: 10.4 us -> 0.01 us  [on_device(): new_object[:, 1, first_row:first_row + slab_total, :] + admm_dual]
    add x6, other arithmetic: 6.61 us -> 15.1 us  [slot_step(): current + weight * object_part]
    slice x7 -> x0, local copies, waits for them, and re-layouts: 8.17 us -> none  [the longest x6 8.04 us: slot_step(): object_patch[0]]
    unnamed x40 -> x48, local copies, waits for them, and re-layouts: 18.8 us -> 11.6 us
    dynamic_update_slice x12 -> x6, local copies, waits for them, and re-layouts: 39.1 us -> 37.5 us  [slot_step(): lax.dynamic_update_slice(grad_sum, current + weight * object_part, anchor)]
  transfers between devices with their start and end apart: 8 -> 8, of which waited for: 5 -> 5; matrix products, arithmetic and copies ran while one was open for 42% -> 40% of each run, Pallas kernels for 0% -> 0%
where the time goes in v1:
time: 610 us; the launch traced here: 607 us
  waiting for transfers between devices  258 us (42%)
  matrix products  150 us (25%)
  local copies, waits for them, and re-layouts  74.5 us (12%)
  other arithmetic  36.4 us (6%)
  loops' own time  32.1 us (5%)
  blocking collectives  24.8 us (4%)
  between operations  17.1 us (3%)
  starting transfers between devices  14.5 us (2%)
    dot_general x97, matrix products, matmul(): return jnp.dot(left, right, preferred_element_type=jnp.float32)  135 us
    psum x1, waiting for transfers between devices, on_device(): probe_flat = lax.psum(probe_flat, ('tile', 'proj', 'cuts'))  128 us
    unnamed x4, waiting for transfers between devices  122 us
    dynamic_update_slice x6, local copies, waits for them, and re-layouts, slot_step(): lax.dynamic_update_slice(grad_sum, current + weight * object_part, anchor)  37.5 us
    another operation x1, loops' own time, on_device(): lax.fori_loop(0, slot_total, lambda slot_index, state_tuple: slot_step(sl...  32.1 us
    all_to_all x1, blocking collectives, on_device(): lax.all_to_all(jnp.stack(jnp.split(slab_values, lax.axis_size('proj'), ax...  24.8 us
    add x6, other arithmetic, slot_step(): current + weight * object_part  15.1 us
  transfers between devices with their start and end apart: 8, of which 5 were waited for; matrix products, arithmetic and copies ran while one was open for 40% of the time, Pallas kernels for 0%

profile of v1, /device:TPU:1, one launch (start us, length us, event | category | flops | bytes accessed | tf_op | source)
XLA Modules:
  0.0 606.9 jit_solution(2859612051960517087)
XLA Ops:
  11.6 5.4 collective-permute-start
  23.4 3.4 mul.431
  26.8 3.3 convolution_bitcast_fusion
  30.1 5.3 copy.57
  36.5 3.1 pad_maximum_fusion
  41.2 231.7 %while.23 = (s32[]{:T(128)}, f32[2,384,768]{2,1,0:T(8,128)}, f32[2,256,256]{2,1,0:T(8,128)}, f32[]{:T(128)}, s32[1,1,6]{2,1,0:T(1,128)S(1)}, /*index=5*/s32[1,1,...) while((s32[]{:T(128)}, f32[2,384,768]{2,1,0:T(8,128)}, ...), condition=%wide.region_2.3_spmd.clone.clone, body=%wide.region_0.2_spmd.clone.clone.sunk | while | flops 558956544 | bytes 15860098 | solution.py:118
  65.8 3.9 add_bitcast_fusion.4
  72.8 6.4 %dynamic_update_slice.13 = f32[2,384,768]{2,1,0:T(8,128)} dynamic-update-slice(f32[2,384,768]{2,1,0:T(8,128)} %get-tuple-element.624, f32[2,256,256]{2,1,0:T(8,128)S(1)} %get-tuple-element.602, s32[]{:T(128)} %constant.167.clone.1..sunk, s32[]{:T(128)S(6)} %select_n.153, s32[]{:T(128)S(6)} %select_n.154) | dynamic-update-slice | bytes 1048580 | tf_op jit(solution)/shard_map/while/body/eval_jaxpr/dynamic_update_slice | solution.py:110
  104.3 3.9 add_bitcast_fusion.4
  108.9 2.5 fusion.215
  111.5 6.2 %dynamic_update_slice.13 = f32[2,384,768]{2,1,0:T(8,128)} dynamic-update-slice(f32[2,384,768]{2,1,0:T(8,128)} %get-tuple-element.624, f32[2,256,256]{2,1,0:T(8,128)S(1)} %get-tuple-element.602, s32[]{:T(128)} %constant.167.clone.1..sunk, s32[]{:T(128)S(6)} %select_n.153, s32[]{:T(128)S(6)} %select_n.154) | dynamic-update-slice | bytes 1048580 | tf_op jit(solution)/shard_map/while/body/eval_jaxpr/dynamic_update_slice | solution.py:110
  143.0 3.9 add_bitcast_fusion.4
  147.6 2.5 fusion.215
  150.1 6.1 %dynamic_update_slice.13 = f32[2,384,768]{2,1,0:T(8,128)} dynamic-update-slice(f32[2,384,768]{2,1,0:T(8,128)} %get-tuple-element.624, f32[2,256,256]{2,1,0:T(8,128)S(1)} %get-tuple-element.602, s32[]{:T(128)} %constant.167.clone.1..sunk, s32[]{:T(128)S(6)} %select_n.153, s32[]{:T(128)S(6)} %select_n.154) | dynamic-update-slice | bytes 1048580 | tf_op jit(solution)/shard_map/while/body/eval_jaxpr/dynamic_update_slice | solution.py:110
  181.4 3.9 add_bitcast_fusion.4
  186.0 2.5 fusion.215
  188.6 6.2 %dynamic_update_slice.13 = f32[2,384,768]{2,1,0:T(8,128)} dynamic-update-slice(f32[2,384,768]{2,1,0:T(8,128)} %get-tuple-element.624, f32[2,256,256]{2,1,0:T(8,128)S(1)} %get-tuple-element.602, s32[]{:T(128)} %constant.167.clone.1..sunk, s32[]{:T(128)S(6)} %select_n.153, s32[]{:T(128)S(6)} %select_n.154) | dynamic-update-slice | bytes 1048580 | tf_op jit(solution)/shard_map/while/body/eval_jaxpr/dynamic_update_slice | solution.py:110
  220.0 3.9 add_bitcast_fusion.4
  224.6 2.5 fusion.215
  227.1 6.3 %dynamic_update_slice.13 = f32[2,384,768]{2,1,0:T(8,128)} dynamic-update-slice(f32[2,384,768]{2,1,0:T(8,128)} %get-tuple-element.624, f32[2,256,256]{2,1,0:T(8,128)S(1)} %get-tuple-element.602, s32[]{:T(128)} %constant.167.clone.1..sunk, s32[]{:T(128)S(6)} %select_n.153, s32[]{:T(128)S(6)} %select_n.154) | dynamic-update-slice | bytes 1048580 | tf_op jit(solution)/shard_map/while/body/eval_jaxpr/dynamic_update_slice | solution.py:110
  258.7 3.9 add_bitcast_fusion.4
  263.3 2.5 fusion.215
  265.8 6.3 %dynamic_update_slice.13 = f32[2,384,768]{2,1,0:T(8,128)} dynamic-update-slice(f32[2,384,768]{2,1,0:T(8,128)} %get-tuple-element.624, f32[2,256,256]{2,1,0:T(8,128)S(1)} %get-tuple-element.602, s32[]{:T(128)} %constant.167.clone.1..sunk, s32[]{:T(128)S(6)} %select_n.153, s32[]{:T(128)S(6)} %select_n.154) | dynamic-update-slice | bytes 1048580 | tf_op jit(solution)/shard_map/while/body/eval_jaxpr/dynamic_update_slice | solution.py:110
  274.9 3.1 collective-permute-start.2
  290.9 24.8 %all_to_all.14 = f32[16,1,1024]{2,1,0:T(1,128)S(1)} all-to-all(f32[16,1,1024]{2,1,0:T(1,128)S(1)} %reshape.143), channel_id=1, replica_groups=mesh['tile'=4,'proj'=16,'cuts'=4] {'proj'}, dimensions={0} | all-to-all | bytes 131072 | tf_op jit(solution)/shard_map/all_to_all | solution.py:144
  318.2 3.3 all-to-all-start.1
  322.8 3.7 all-to-all-done.1
  327.6 121.8 %reduce-scatter.4.cloned.1.call-done = f32[32,512]{1,0:T(8,128)} async-done(((f32[2048,512]{1,0:T(8,128)}), f32[32,512]{1,0:T(8,128)}) %reduce-scatter.4.cloned.1.call-update) | async-done | bytes 65552
  451.2 128.4 %all-reduce.3.cloned.1.call-done = f32[131200]{0:T(1024)} async-done(((f32[131200]{0:T(1024)}), f32[131200]{0:T(1024)}) %all-reduce.3.cloned.1.call-update) | async-done | bytes 524816 | tf_op jit(solution)/shard_map/psum | solution.py:133
  585.4 2.9 convolution_bitcast_fusion.2
  590.8 3.8 fusion.116
  594.7 4.7 convolution_subtract_fusion.4
  (201 shorter events, 166.8 us)
Async XLA Ops:
  8.0 18.8 %copy-start = (bf16[16,32,2048]{2,1,0:T(8,128)(2,1)S(1)}, bf16[16,32,2048]{2,1,0:T(8,128)(2,1)}, u32[]{:S(2)}) copy-start(bf16[16,32,2048]{2,1,0:T(8,128)(2,1)} %param.25) | copy-start | bytes 6291460
  8.0 441.4 %reduce-scatter.4.cloned.1.call-start = ((), (), s32[]{:S(2)}) async-start(), calls=%async_computation.5 | async-start | bytes 4259840
  8.1 11.9 %copy-start.3 = (f32[8,32,2048]{2,1,0:T(8,128)S(1)}, f32[8,32,2048]{2,1,0:T(8,128)}, u32[]{:S(2)}) copy-start(f32[8,32,2048]{2,1,0:T(8,128)} %param.24) | copy-start | bytes 6291460
  10.3 26.2 %collective-permute-start.1 = (f32[2,384,128]{2,1,0:T(8,128)}, f32[2,384,128]{2,1,0:T(8,128)S(1)}, u32[]{:S(2)}, u32[]{:S(2)}) collective-permute-start(f32[2,384,128]{2,1,0:T(8,128)} %get-tuple-element.513), channel_id=1, source_target_pairs={{64,0},{128,64},{192,128},{65,1},{129,65},{193,129},{66,2},{130,66... | collective-permute-start | bytes 1179656 | tf_op jit(solution)/shard_map/ppermute | solution.py:14
  11.6 24.9 %collective-permute-start = (f32[2,384,128]{2,1,0:T(8,128)}, f32[2,384,128]{2,1,0:T(8,128)}, u32[]{:S(2)}, u32[]{:S(2)}) collective-permute-start(f32[2,384,128]{2,1,0:T(8,128)} %get-tuple-element.512), channel_id=1, source_target_pairs={{0,64},{64,128},{128,192},{1,65},{65,129},{129,193},{2,66},{66,130... | collective-permute-start | bytes 1179656 | tf_op jit(solution)/shard_map/ppermute | solution.py:14
  19.1 0.8 copy-start.6
  35.4 1.0 copy-start.4
  39.6 1.6 copy-start.11
  39.6 1.6 copy-start.12
  274.9 10.6 %collective-permute-start.2 = (f32[2,384,128]{2,1,0:T(8,128)}, f32[2,384,128]{2,1,0:T(8,128)S(1)}, u32[]{:S(2)}, u32[]{:S(2)}) collective-permute-start(f32[2,384,128]{2,1,0:T(8,128)} %get-tuple-element.511), channel_id=1, source_target_pairs={{0,64},{64,128},{128,192},{1,65},{65,129},{129,193},{2,66},{66,130... | collective-permute-start | bytes 1179656 | tf_op jit(solution)/shard_map/ppermute | solution.py:14
  278.0 10.1 %collective-permute-start.3 = (f32[2,384,128]{2,1,0:T(8,128)S(1)}, f32[2,384,128]{2,1,0:T(8,128)S(1)}, u32[]{:S(2)}, u32[]{:S(2)}) collective-permute-start(f32[2,384,128]{2,1,0:T(8,128)S(1)} %get-tuple-element.510), channel_id=1, source_target_pairs={{64,0},{128,64},{192,128},{65,1},{129,65},{193,129},{66,2},{130,66... | collective-permute-start | bytes 1179656 | tf_op jit(solution)/shard_map/ppermute | solution.py:14
  281.7 6.6 %copy-start.2 = (f32[1,2,384,512]{3,2,1,0:T(8,128)S(1)}, f32[1,2,384,512]{3,2,1,0:T(8,128)}, u32[]{:S(2)}) copy-start(f32[1,2,384,512]{3,2,1,0:T(8,128)} %param.17) | copy-start | bytes 4718596
  288.3 1.6 copy-start.9
  288.7 1.1 copy-start.8
  289.8 31.7 %copy-start.1 = (f32[2,256,256]{2,1,0:T(8,128)S(1)}, f32[2,256,256]{2,1,0:T(8,128)}, u32[]{:S(2)}) copy-start(f32[2,256,256]{2,1,0:T(8,128)} %get-tuple-element.383) | copy-start | bytes 1572868
  318.2 8.3 %all-to-all-start.1 = ((f32[4,1,4096]{2,1,0:T(1,128)}), f32[4,1,4096]{2,1,0:T(1,128)S(1)}, u32[]{:S(2)}, u32[]{:S(2)}) async-start(f32[4,1,4096]{2,1,0:T(1,128)} %reshape.145), calls=%async_computation.1 | async-start | bytes 131072 | tf_op jit(solution)/shard_map/all_to_all | solution.py:142
  321.5 258.1 %all-reduce.3.cloned.1.call-start = ((), (), s32[]{:S(2)}) async-start(), calls=%async_computation.3 | async-start | bytes 1056768 | tf_op jit(solution)/shard_map/psum | solution.py:133
  321.9 129.3 %copy-start.10 = (s32[64]{0:T(128)S(1)}, s32[64]{0:T(128)}, u32[]{:S(2)}) copy-start(s32[64]{0:T(128)} %param.27) | copy-start | bytes 772
  322.7 262.6 %all-gather.2.cloned.1.call-start = ((), (), s32[]{:S(2)}) async-start(), calls=%async_computation.4 | async-start | bytes 2129920 | tf_op jit(solution)/shard_map/all_gather | solution.py:185
  327.3 257.2 %copy-start.5 = (f32[2,256,256]{2,1,0:T(8,128)S(1)}, f32[2,256,256]{2,1,0:T(8,128)}, u32[]{:S(2)}) copy-start(f32[2,256,256]{2,1,0:T(8,128)} %param.18) | copy-start | bytes 1572868
  590.8 4.0 copy-start.7
Sparse Core Ops, SparseCore 0:
  35.6 413.7 reduce-scatter.3
  452.9 85.0 all-gather.1
Sparse Core Ops, SparseCore 1:
  328.1 251.4 all-reduce.2
